TPU v7x, 512 devices: a whole 4x8x8 slice. The times are simulated.
512 devices in a mesh: space: 32 (over y_lo, z), chaos: 16 (over x, y_hi, core).
Axes of the slice: x: 4, y: 8 (y_hi: 2, y_lo: 4; y = y_hi * 4 + y_lo), z: 8, core: 2. Of those that a mesh axis runs over, the one named last changes fastest.
Arguments:
- load_vectors: bfloat16 [256, 2, 16, 12288], P('chaos', None, None, 'space'), may hold values from -6 to 6
- stiff_tiles: bfloat16 [128, 3, 8, 2, 96, 96], P('space'), may hold values from -0.09375 to 0.09375
- tile_columns: int32 [128, 3], P('space'), may hold values from 0 to 5, as said below
- chaos_index: int32 [8, 256, 32], replicated, may hold values from 0 to 255, as said below
- chaos_value: bfloat16 [8, 256, 32], replicated, may hold values from -1 to 1
Outputs:
- response: float32 [256, 2, 16, 12288], P('chaos', None, None, 'space')
Inputs may be any that keep to these rules, and one draw needn't show every extreme that they name: `tile_columns`: in row b of one subdomain with local index l = b % 4, the three numbers are l + 1, one of 0 to l, and one of l + 2 to 5. `chaos_index`: for every k and i the 32 numbers are distinct and the first is i.
All inputs are finite; a program needn't handle non-finite values.
Results may differ from a plain program's by a relative error of at most 0.0029.
Values may be sent and summed in bfloat16 or wider, within the bound.
A program may use at most 128 MiB of HBM per device.

v0:
```python
import jax
import jax.numpy as jnp
from jax import lax
from jax.sharding import PartitionSpec as P

TILE = 96
NKL = 8
P_SIZE = 256


def with_halo(cells, sides, width):
    for axis, dim in sides:
        count = lax.axis_size(axis)
        ends = count - 1
        head = lax.slice_in_dim(cells, 0, width, axis=dim)
        tail = lax.slice_in_dim(cells, cells.shape[dim] - width, cells.shape[dim], axis=dim)
        cells = jnp.concatenate(
            [
                lax.ppermute(tail, axis, [(i, (i + 1) % count) for i in range(ends)]),
                cells,
                lax.ppermute(head, axis, [((i + 1) % count, i) for i in range(ends)]),
            ],
            axis=dim,
        )
    return cells


def dense_coupling(chaos_index, chaos_value):
    columns = jnp.arange(P_SIZE, dtype=jnp.int32)

    def one_term(index_pair):
        row_index, row_value = index_pair
        matches = row_index[:, :, None] == columns[None, None, :]
        summed = jnp.where(matches, row_value[:, :, None], jnp.zeros((), jnp.bfloat16)).sum(axis=1)
        return summed

    return lax.map(one_term, (chaos_index, chaos_value))


def body(load_vectors, stiff_tiles, tile_columns, chaos_index, chaos_value):
    extended = with_halo(load_vectors, (("space", 3),), TILE)
    own_terms = load_vectors.shape[0]
    blocks = stiff_tiles.shape[0]
    first_term = lax.axis_index("chaos") * own_terms
    own_index = lax.dynamic_slice_in_dim(chaos_index, first_term, own_terms, 1)
    own_value = lax.dynamic_slice_in_dim(chaos_value, first_term, own_terms, 1)
    coupling = dense_coupling(own_index, own_value)
    coupled_field = jnp.einsum(
        "kij,jcre->kicre",
        coupling,
        lax.all_gather(extended, "chaos", axis=0, tiled=True),
        preferred_element_type=jnp.float32,
    ).astype(jnp.bfloat16)
    terms = coupled_field.shape[1]
    cases = coupled_field.shape[3]
    coupled_field = coupled_field.reshape(NKL, terms, 2, cases, blocks + 2, TILE)
    real_part = stiff_tiles[:, :, :, 0]
    imag_part = stiff_tiles[:, :, :, 1]
    upper_row = jnp.stack([real_part, -imag_part], axis=3)
    lower_row = jnp.stack([imag_part, real_part], axis=3)
    complex_tiles = jnp.stack([upper_row, lower_row], axis=3)
    accum_sum = jnp.zeros((terms, 2, cases, blocks, TILE), jnp.float32)
    for tile_slot in range(stiff_tiles.shape[1]):
        columns = jnp.take(coupled_field, tile_columns[:, tile_slot], axis=4)
        accum_sum = accum_sum + jnp.einsum(
            "bkcdxy,kidrby->icrbx",
            complex_tiles[:, tile_slot],
            columns,
            preferred_element_type=jnp.float32,
        )
    result = accum_sum.reshape(terms, 2, cases, blocks * TILE)
    return result


def solution(mesh):
    in_specs = (
        P("chaos", None, None, "space"),
        P("space", None, None, None, None, None),
        P("space", None),
        P(),
        P(),
    )
    out_specs = P("chaos", None, None, "space")
    return jax.shard_map(body, mesh=mesh, in_specs=in_specs, out_specs=out_specs, check_vma=False)
```

profile of v0, /device:TPU:9, one launch (start us, length us, event | category | flops | bytes accessed | tf_op | source)
XLA Modules:
  0.0 222.4 jit_solution(17434653015442165927)
XLA Ops:
  6.5 1.2 copy.32
  7.8 10.6 %collective-permute-start.1 = (bf16[16,2,16,96]{3,0,2,1:T(8,128)(2,1)S(1)}, bf16[16,2,16,96]{3,0,2,1:T(8,128)(2,1)S(1)}, u32[]{:S(2)}, u32[]{:S(2)}) collective-permute-start(bf16[16,2,16,96]{3,0,2,1:T(8,128)(2,1)S(1)} %get-tuple-element.96), channel_id=1, source_target_pairs={{16,0},{32,16},{48,32},{64,48},{80,64},{96,80},{112,96},{128,112},... | collective-permute-start | bytes 294920 | tf_op jit(solution)/shard_map/ppermute | solution.py:21
  18.4 1.9 collective-permute-start
  20.5 5.7 %collective-permute-done = bf16[16,2,16,96]{3,0,2,1:T(8,128)(2,1)S(1)} collective-permute-done((bf16[16,2,16,96]{3,0,2,1:T(8,128)(2,1)S(1)}, bf16[16,2,16,96]{3,0,2,1:T(8,128)(2,1)S(1)}, u32[]{:S(2)}, u32[]{:S(2)}) %collective-permute-start) | collective-permute-done | bytes 98336 | tf_op jit(solution)/shard_map/ppermute | solution.py:19
  26.2 1.2 pad_maximum_fusion.2
  27.6 0.9 constant_dynamic-slice_fusion
  28.7 1.0 slice_reduce_fusion
  29.8 3.3 %fusion.58 = (bf16[4,3,8,1,96,96]{5,4,3,2,1,0:T(8,128)(2,1)S(1)}, bf16[4,3,8,1,96,96]{5,4,3,2,1,0:T(8,128)(2,1)S(1)}) fusion(bf16[4,3,8,2,96,96]{5,4,3,2,1,0:T(8,128)(2,1)} %param.10), kind=kLoop, calls=%fused_computation.62 | loop fusion | bytes 7077888 | tf_op jit(solution)/shard_map/slice | solution.py:57
  33.0 0.3 copy_negate_fusion
  33.3 5.0 %maximum_bitcast_fusion = (bf16[4,3,8,1,2,96,96]{6,5,2,4,3,0,1:T(8,128)(2,1)}, bf16[4,3,8,1,2,96,96]{6,5,2,4,3,0,1:T(8,128)(2,1)}) fusion(bf16[4,3,8,1,96,96]{5,4,2,3,0,1:T(8,128)(2,1)S(1)} %copy_negate_fusion, bf16[4,3,8,1,96,96]{5,4,3,2,1,0:T(8,128)(2,1)S(1)} %get-tuple-element.93, bf16[4,3,8,1,96,96]{5,4,3,2,1,0:T(8,128)(2,1)S(1)} %get-tuple-element.94), kind=kLoop, calls=%fused_computation.16 | loop fusion | flops 8847360 | bytes 12386304 | tf_op jit(solution)/shard_map/stack | solution.py:61
  38.4 2.4 %while.13 = (s32[]{:T(128)}, bf16[8,16,256]{2,1,0:T(8,128)(2,1)S(1)}, s32[8,16,32]{2,1,0:T(8,128)S(1)}, bf16[8,16,32]{2,1,0:T(8,128)(2,1)S(1)}, s32[]{:T(128)}) while((s32[]{:T(128)}, bf16[8,16,256]{2,1,0:T(8,128)(2,1)S(1)}, s32[8,16,32]{2,1,0:T(8,128)S(1)}, bf16[8,16,32]{2,1,0:T(8,128)(2,1)S(1)}, s32[]{:T(128)}) %tuple.37), condition=%wide.region_2.3_spmd.clone, body=%wide.region_0.2_spmd.clone.sunk | while | flops 389122 | bytes 33873 | solution.py:37
  40.8 113.3 %all-gather.2.cloned.1.call-done = bf16[256,2,16,576]{3,0,2,1:T(8,128)(2,1)} async-done(((bf16[16,2,16,576]{3,0,2,1:T(8,128)(2,1)}), bf16[256,2,16,576]{3,0,2,1:T(8,128)(2,1)}) %all-gather.2.cloned.1.call-update) | async-done | bytes 9437200 | tf_op jit(solution)/shard_map/all_gather | solution.py:51
  154.0 7.9 %fusion.21 = bf16[8,16,2,16,576]{4,1,3,2,0:T(8,128)(2,1)} fusion(bf16[256,2,16,576]{3,0,2,1:T(8,128)(2,1)} %all-gather.2.cloned.1.call-done, bf16[8,16,256]{2,1,0:T(8,128)(2,1)S(1)} %get-tuple-element.71), kind=kOutput, calls=%fused_computation.35 | convolution fusion | flops 1210318848 | bytes 14221312 | tf_op jit(solution)/shard_map/kij,jcre->kicre/dot_general | solution.py:48
  161.9 13.6 %reshape.62 = bf16[8,16,2,16,6,96]{5,4,1,3,2,0:T(8,128)(2,1)} reshape(bf16[8,16,2,16,576]{4,1,3,2,0:T(8,128)(2,1)} %fusion.21) | data formatting | bytes 9437184 | tf_op jit(solution)/shard_map/reshape | solution.py:56
  175.5 10.1 %copy.36 = bf16[8,16,2,16,6,96]{5,3,2,1,0,4:T(8,128)(2,1)} copy(bf16[8,16,2,16,6,96]{5,4,1,3,2,0:T(8,128)(2,1)} %reshape.62) | data formatting | bytes 9437184 | tf_op jit(solution)/shard_map/reshape | solution.py:56
  185.7 5.8 %gather_fusion = bf16[4,8,16,2,16,96]{5,4,3,2,1,0:T(8,128)(2,1)} fusion(bf16[8,16,2,16,6,96]{5,3,2,1,0,4:T(8,128)(2,1)} %copy.36, s32[1024]{0:T(1024)S(1)} %pad_clamp_fusion.2), kind=kCustom, calls=%fused_computation.clone | custom fusion | bytes 6291472 | tf_op jit(solution)/shard_map/jit(_take)/gather | solution.py:64
  191.5 5.8 %gather_fusion.1 = bf16[4,8,16,2,16,96]{5,4,3,2,1,0:T(8,128)(2,1)} fusion(bf16[8,16,2,16,6,96]{5,3,2,1,0,4:T(8,128)(2,1)} %copy.36, s32[1024]{0:T(1024)S(1)} %pad_clamp_fusion.1), kind=kCustom, calls=%fused_computation.1.clone | custom fusion | bytes 6291472 | tf_op jit(solution)/shard_map/jit(_take)/gather | solution.py:64
  197.3 5.9 %gather_fusion.2 = bf16[4,8,16,2,16,96]{5,4,3,2,1,0:T(8,128)(2,1)} fusion(bf16[8,16,2,16,6,96]{5,3,2,1,0,4:T(8,128)(2,1)} %copy.36, s32[1024]{0:T(1024)S(1)} %pad_clamp_fusion), kind=kCustom, calls=%fused_computation.2.clone | custom fusion | bytes 6291472 | tf_op jit(solution)/shard_map/jit(_take)/gather | solution.py:64
  203.2 4.6 %fusion.24 = f32[4,16,16,2,96]{4,2,3,1,0:T(8,128)S(1)} fusion(bf16[4,3,8,1,2,96,96]{6,5,2,4,3,0,1:T(8,128)(2,1)} %get-tuple-element.101, bf16[4,3,8,1,2,96,96]{6,5,2,4,3,0,1:T(8,128)(2,1)} %get-tuple-element.102, bf16[4,8,16,2,16,96]{5,4,3,2,1,0:T(8,128)(2,1)} %gather_fusion, pred[4]{0:T(512)(128)(4,1)S(1)} %compare_and_fusion.2), kind=kOutput, calls=%fused_computation.37 | convolution fusion | flops 610271232 | bytes 11010052 | tf_op jit(solution)/shard_map/bkcdxy,kidrby->icrbx/dot_general | solution.py:65
  207.8 1.0 copy-done.3
  208.8 3.1 %fusion.49 = f32[4,16,16,2,96]{4,2,3,1,0:T(8,128)S(1)} fusion(f32[4,16,16,2,96]{4,2,3,1,0:T(8,128)S(1)} %fusion.24, bf16[4,3,8,1,2,96,96]{6,5,2,4,3,0,1:T(8,128)(2,1)S(1)} %bitcast.101, bf16[4,3,8,1,2,96,96]{6,5,2,4,3,0,1:T(8,128)(2,1)} %get-tuple-element.102, bf16[4,8,16,2,16,96]{5,4,3,2,1,0:T(8,128)(2,1)S(1)} %copy-done.3, ...), kind=kOutput, calls=%fused_computation.42 | convolution fusion | flops 610467840 | bytes 11796484 | tf_op jit(solution)/shard_map/bkcdxy,kidrby->icrbx/dot_general | solution.py:65
  212.1 1.4 fusion.44
  213.4 0.7 copy.45
  214.2 1.4 reshape.17
  (64 shorter events, 2.9 us)
Async XLA Ops:
  6.5 20.9 %copy-start = (s32[8,256,32]{1,2,0:T(8,128)S(1)}, s32[8,256,32]{1,2,0:T(8,128)}, u32[]{:S(2)}) copy-start(s32[8,256,32]{1,2,0:T(8,128)} %param.12) | copy-start | bytes 786436
  6.5 147.5 %all-gather.2.cloned.1.call-start = ((), (), s32[]{:S(2)}) async-start(), calls=%async_computation | async-start | bytes 11141120 | tf_op jit(solution)/shard_map/all_gather | solution.py:51
  7.8 12.7 %collective-permute-start.1 = (bf16[16,2,16,96]{3,0,2,1:T(8,128)(2,1)S(1)}, bf16[16,2,16,96]{3,0,2,1:T(8,128)(2,1)S(1)}, u32[]{:S(2)}, u32[]{:S(2)}) collective-permute-start(bf16[16,2,16,96]{3,0,2,1:T(8,128)(2,1)S(1)} %get-tuple-element.96), channel_id=1, source_target_pairs={{16,0},{32,16},{48,32},{64,48},{80,64},{96,80},{112,96},{128,112},... | collective-permute-start | bytes 294920 | tf_op jit(solution)/shard_map/ppermute | solution.py:21
  18.4 7.8 %collective-permute-start = (bf16[16,2,16,96]{3,0,2,1:T(8,128)(2,1)S(1)}, bf16[16,2,16,96]{3,0,2,1:T(8,128)(2,1)S(1)}, u32[]{:S(2)}, u32[]{:S(2)}) collective-permute-start(bf16[16,2,16,96]{3,0,2,1:T(8,128)(2,1)S(1)} %get-tuple-element.95), channel_id=1, source_target_pairs={{0,16},{16,32},{32,48},{48,64},{64,80},{80,96},{96,112},{112,128},... | collective-permute-start | bytes 294920 | tf_op jit(solution)/shard_map/ppermute | solution.py:19
  197.3 10.5 %slice-start = ((s8[4718592]{0:T(1024)(128)(4,1)}), s8[524288]{0:T(1024)(128)(4,1)S(1)}, s32[]{:S(2)}) async-start(s8[4718592]{0:T(1024)(128)(4,1)} %bitcast.100), calls=%async_computation.1 | async-start | bytes 1048576
  203.2 4.6 %slice-start.1 = ((s8[4718592]{0:T(1024)(128)(4,1)}), s8[4194304]{0:T(1024)(128)(4,1)S(1)}, s32[]{:S(2)}) async-start(s8[4718592]{0:T(1024)(128)(4,1)} %bitcast.100), calls=%async_computation.2 | async-start | bytes 8388608
  203.2 5.6 %copy-start.3 = (bf16[4,8,16,2,16,96]{5,4,3,2,1,0:T(8,128)(2,1)S(1)}, bf16[4,8,16,2,16,96]{5,4,3,2,1,0:T(8,128)(2,1)}, u32[]{:S(2)}) copy-start(bf16[4,8,16,2,16,96]{5,4,3,2,1,0:T(8,128)(2,1)} %gather_fusion.1) | copy-start | bytes 9437188
  203.2 8.8 %slice-start.2 = ((s8[4718592]{0:T(1024)(128)(4,1)}), s8[4194304]{0:T(1024)(128)(4,1)S(1)}, s32[]{:S(2)}) async-start(s8[4718592]{0:T(1024)(128)(4,1)} %bitcast.102), calls=%async_computation.3 | async-start | bytes 8388608
  208.8 3.1 %slice-start.3 = ((s8[4718592]{0:T(1024)(128)(4,1)}), s8[524288]{0:T(1024)(128)(4,1)S(1)}, s32[]{:S(2)}) async-start(s8[4718592]{0:T(1024)(128)(4,1)} %bitcast.102), calls=%async_computation.4 | async-start | bytes 1048576
  208.8 3.2 %copy-start.2 = (bf16[4,8,16,2,16,96]{5,4,3,2,1,0:T(8,128)(2,1)S(1)}, bf16[4,8,16,2,16,96]{5,4,3,2,1,0:T(8,128)(2,1)}, u32[]{:S(2)}) copy-start(bf16[4,8,16,2,16,96]{5,4,3,2,1,0:T(8,128)(2,1)} %gather_fusion.2) | copy-start | bytes 9437188
  212.1 3.5 %copy-start.1 = (s32[8,256,32]{1,2,0:T(8,128)S(1)}, s32[8,256,32]{1,2,0:T(8,128)}, u32[]{:S(2)}) copy-start(s32[8,256,32]{1,2,0:T(8,128)} %param.12) | copy-start | bytes 786436
Sparse Core Ops, SparseCore 0:
  27.5 126.4 all-gather.1
where the time goes:
time: 223 us; the launch traced here: 222 us
  waiting for transfers between devices  119 us (53%)
  local copies, waits for them, and re-layouts  51.5 us (23%)
  matrix products  16.9 us (8%)
  between operations  13.6 us (6%)
  starting transfers between devices  12.5 us (6%)
  other arithmetic  8.46 us (4%)
    all_gather x1, waiting for transfers between devices, body(): lax.all_gather(extended, 'chaos', axis=0, tiled=True)  113 us
    reshape x2, local copies, waits for them, and re-layouts, body(): coupled_field.reshape(NKL, terms, 2, cases, blocks + 2, TILE)  23.7 us
    gather x3, local copies, waits for them, and re-layouts, body(): columns = jnp.take(coupled_field, tile_columns[:, tile_slot], axis=4)  17.5 us
    ppermute x1, starting transfers between devices, with_halo(): lax.ppermute(head, axis, [((i + 1) % count, i) for i in range(ends)])  10.6 us
    dot_general x3, matrix products, body(): jnp.einsum('bkcdxy,kidrby->icrbx', complex_tiles[:, tile_slot], columns,...  9.03 us
    dot_general x1, matrix products, body(): jnp.einsum('kij,jcre->kicre', coupling, lax.all_gather(extended, 'chaos',...  7.9 us
    ppermute x1, waiting for transfers between devices, with_halo(): lax.ppermute(tail, axis, [(i, (i + 1) % count) for i in range(ends)])  5.66 us
    another operation x1, other arithmetic, body(): complex_tiles = jnp.stack([upper_row, lower_row], axis=3)  5.02 us
  transfers between devices with their start and end apart: 3, of which 3 were waited for; matrix products, arithmetic and copies ran while one was open for 6% of the time, Pallas kernels for 0%

commit v1 on v0

v1 whole, which is shorter than its diff:
```python
import functools

import jax
import jax.numpy as jnp
from jax import lax
from jax.experimental import pallas as pl
from jax.experimental.pallas import tpu as pltpu
from jax.sharding import PartitionSpec as P

MESH = pl.DeviceIdType.MESH
TILE = 96
LANE = 128
NKL = 8
NNZ = 3
FAR = (15, 14, 11, 10, 7, 6, 3, 2)
NEAR = (13, 12, 9, 8, 5, 4, 1)
ORDER = FAR + NEAR


def kernel(
    spaces,
    cols,
    xt,
    st,
    ci,
    cv,
    out,
    got,
    left_halo,
    right_halo,
    tiles,
    coup,
    weights,
    xcat,
    mixed,
    result,
    st_sem,
    own_sem,
    in_send,
    in_recv,
    halo_send,
    halo_recv,
    out_send,
    out_recv,
):
    s, c = lax.axis_index("space"), lax.axis_index("chaos")
    has_left, has_right = s > 0, s < spaces - 1
    load_tiles = pltpu.make_async_copy(st, tiles, st_sem)
    load_tiles.start()
    own_in = pltpu.make_async_copy(xt.at[c], got.at[c], own_sem.at[0])
    own_in.start()

    barrier = pltpu.get_barrier_semaphore()
    for k in ORDER:
        pl.semaphore_signal(barrier, inc=1, device_id=(s, c ^ k), device_id_type=MESH)

    @pl.when(has_left)
    def _():
        pl.semaphore_signal(barrier, inc=1, device_id=(s - 1, c), device_id_type=MESH)

    @pl.when(has_right)
    def _():
        pl.semaphore_signal(barrier, inc=1, device_id=(s + 1, c), device_id_type=MESH)

    pl.semaphore_wait(barrier, 15 + has_left.astype(jnp.int32) + has_right.astype(jnp.int32))

    sends = [
        pltpu.make_async_remote_copy(
            xt.at[c ^ k], got.at[c], in_send.at[k], in_recv.at[k], device_id=(s, c ^ k), device_id_type=MESH
        )
        for k in ORDER
    ]
    for copy in sends:
        copy.start()

    def one_coupling(step, _):
        k, half = step // 2, step % 2
        rows = lax.broadcasted_iota(jnp.int32, (LANE, 256), 0) + half * LANE
        total = jnp.zeros((LANE, 256), jnp.float32)
        for n in range(32):
            total = jnp.where(ci[k, n : n + 1, :] == rows, cv[k, n : n + 1, :].astype(jnp.float32), total)
        coup[k, half] = total.T.astype(jnp.bfloat16)
        return 0

    lax.fori_loop(0, 2 * NKL, one_coupling, 0)

    load_tiles.wait()

    def one_weight(step, _):
        b, slot = step // NNZ, step % NNZ
        pad = jnp.zeros((TILE, LANE - TILE), jnp.bfloat16)
        for k in range(NKL):
            real = jnp.concatenate([tiles[b, slot, k, 0], pad], axis=1)
            imag = jnp.concatenate([tiles[b, slot, k, 1], pad], axis=1)
            weights[b, slot, 0:TILE, 2 * k * LANE : (2 * k + 1) * LANE] = real
            weights[b, slot, 0:TILE, (2 * k + 1) * LANE : (2 * k + 2) * LANE] = -imag
            weights[b, slot, TILE : 2 * TILE, 2 * k * LANE : (2 * k + 1) * LANE] = imag
            weights[b, slot, TILE : 2 * TILE, (2 * k + 1) * LANE : (2 * k + 2) * LANE] = real
        return 0

    lax.fori_loop(0, 4 * NNZ, one_weight, 0)

    @pl.when(jnp.logical_not(has_left))
    def _():
        left_halo[...] = jnp.zeros_like(left_halo)

    @pl.when(jnp.logical_not(has_right))
    def _():
        right_halo[...] = jnp.zeros_like(right_halo)

    def to_left(k):
        return pltpu.make_async_remote_copy(
            got.at[c ^ k, :, :, pl.ds(0, LANE)],
            right_halo.at[c ^ k],
            halo_send.at[0, k],
            halo_recv.at[0, k],
            device_id=(s - 1, c),
            device_id_type=MESH,
        )

    def to_right(k):
        return pltpu.make_async_remote_copy(
            got.at[c ^ k, :, :, pl.ds(2 * LANE, LANE)],
            left_halo.at[c ^ k],
            halo_send.at[1, k],
            halo_recv.at[1, k],
            device_id=(s + 1, c),
            device_id_type=MESH,
        )

    def pass_on(k):
        @pl.when(has_left)
        def _():
            to_left(k).start()

        @pl.when(has_right)
        def _():
            to_right(k).start()

    own_in.wait()
    pass_on(0)
    arrivals = {k: copy for k, copy in zip(ORDER, sends)}
    for k in NEAR[::-1] + FAR:
        arrivals[k].wait_recv()
        pass_on(k)

    pad = jnp.zeros((256, LANE - TILE), jnp.bfloat16)
    for part in range(2):
        cells = got[:, part].reshape(256, 3 * LANE)
        for b in range(4):
            block = cells[:, b * TILE : b * TILE + LANE] if b < 3 else jnp.concatenate([cells[:, 3 * TILE :], pad], axis=1)
            xcat[:, (2 * (b + 1) + part) * LANE : (2 * (b + 1) + part + 1) * LANE] = block

    yhi = (c // 2) % 2

    def mix(first, count):
        def one_k(k, _):
            matrix = jnp.concatenate([coup[k, 0], coup[k, 1]], axis=1)
            for g in range(first, first + count):
                value = jnp.dot(matrix, xcat[:, 2 * g * LANE : 2 * (g + 1) * LANE], preferred_element_type=jnp.float32)
                value = value.astype(jnp.bfloat16)
                for q in range(8):
                    place = jnp.where(q % 2 == yhi, 4, 0) + q // 2
                    mixed[g, k, pl.ds(pl.multiple_of(place * 32, 32), 32), :] = value[32 * q : 32 * q + 32]
            return 0

        lax.fori_loop(0, NKL, one_k, 0)

    mix(1, 4)

    @pl.when(has_right)
    def _():
        for k in range(16):
            to_left(k).wait_recv()

    @pl.when(has_left)
    def _():
        for k in range(16):
            to_right(k).wait_recv()

    for part in range(2):
        low = left_halo[:, part].reshape(256, LANE)
        xcat[:, part * LANE : (part + 1) * LANE] = jnp.concatenate([low[:, LANE - TILE :], pad], axis=1)
        xcat[:, (10 + part) * LANE : (11 + part) * LANE] = right_halo[:, part].reshape(256, LANE)
    mix(0, 1)
    mix(5, 1)

    def out_copy(k):
        to = c ^ k
        half = 0 if k & 2 else 1
        place = half * 8 + (to // 4) * 2 + to % 2
        return pltpu.make_async_remote_copy(
            result.at[place], out.at[c], out_send.at[k], out_recv.at[k], device_id=(s, to), device_id_type=MESH
        )

    for half in range(2):
        parts = []
        for b in range(4):
            total = jnp.zeros((128, 2 * TILE), jnp.float32)
            for slot in range(NNZ):
                g = cols[b, slot]
                for k in range(NKL):
                    total = total + lax.dot_general(
                        mixed[g, k, 128 * half : 128 * half + 128, :],
                        weights[b, slot, :, 2 * k * LANE : 2 * (k + 1) * LANE],
                        (((1,), (1,)), ((), ())),
                        preferred_element_type=jnp.float32,
                    )
            parts.append(total)
        for part in range(2):
            value = jnp.concatenate([total[:, part * TILE : (part + 1) * TILE] for total in parts], axis=1)
            result[8 * half : 8 * half + 8, part] = value.astype(jnp.bfloat16).reshape(8, 16, 3 * LANE)
        for k in (NEAR if half else FAR):
            out_copy(k).start()
    own_out = pltpu.make_async_copy(result.at[8 + (c // 4) * 2 + c % 2], out.at[c], own_sem.at[1])
    own_out.start()

    for copy in sends:
        copy.wait_send()

    @pl.when(has_left)
    def _():
        for k in range(16):
            to_left(k).wait_send()

    @pl.when(has_right)
    def _():
        for k in range(16):
            to_right(k).wait_send()

    own_out.wait()
    for k in ORDER:
        out_copy(k).wait()


def body(load_vectors, stiff_tiles, tile_columns, chaos_index, chaos_value):
    spaces = lax.axis_size("space")
    xt = jnp.transpose(load_vectors, (2, 1, 0, 3))
    ci = jnp.transpose(chaos_index, (0, 2, 1))
    cv = jnp.transpose(chaos_value, (0, 2, 1))
    vmem, hbm = pl.BlockSpec(memory_space=pltpu.VMEM), pl.BlockSpec(memory_space=pl.ANY)
    bf16 = jnp.bfloat16
    out = pl.pallas_call(
        functools.partial(kernel, spaces),
        out_shape=jax.ShapeDtypeStruct((16, 2, 16, 384), bf16),
        in_specs=[pl.BlockSpec(memory_space=pltpu.SMEM), hbm, hbm, vmem, vmem],
        out_specs=hbm,
        scratch_shapes=[
            pltpu.VMEM((16, 2, 16, 384), bf16),
            pltpu.VMEM((16, 2, 16, LANE), bf16),
            pltpu.VMEM((16, 2, 16, LANE), bf16),
            pltpu.VMEM(stiff_tiles.shape, bf16),
            pltpu.VMEM((NKL, 2, 256, LANE), bf16),
            pltpu.VMEM((4, NNZ, 2 * TILE, 2 * NKL * LANE), bf16),
            pltpu.VMEM((256, 12 * LANE), bf16),
            pltpu.VMEM((6, NKL, 256, 2 * LANE), bf16),
            pltpu.VMEM((16, 2, 16, 384), bf16),
            pltpu.SemaphoreType.DMA,
            pltpu.SemaphoreType.DMA((2,)),
            pltpu.SemaphoreType.DMA((16,)),
            pltpu.SemaphoreType.DMA((16,)),
            pltpu.SemaphoreType.DMA((2, 16)),
            pltpu.SemaphoreType.DMA((2, 16)),
            pltpu.SemaphoreType.DMA((16,)),
            pltpu.SemaphoreType.DMA((16,)),
        ],
        compiler_params=pltpu.CompilerParams(collective_id=0, has_side_effects=True, vmem_limit_bytes=60 * 1024 * 1024),
    )(tile_columns, xt, stiff_tiles, ci, cv)
    return jnp.transpose(out, (2, 1, 0, 3)).astype(jnp.float32)


def solution(mesh):
    in_specs = (
        P("chaos", None, None, "space"),
        P("space", None, None, None, None, None),
        P("space", None),
        P(),
        P(),
    )
    out_specs = P("chaos", None, None, "space")
    return jax.shard_map(body, mesh=mesh, in_specs=in_specs, out_specs=out_specs, check_vma=False)
```

time: 223 us -> 54.1 us (0.24)
  the two profiles are of different devices: /device:TPU:9 before, /device:TPU:24 now
where the time goes in v1:
time: 54.1 us; the launch traced here: 53.9 us
  Pallas kernels  49.6 us (92%)
  local copies, waits for them, and re-layouts  3.21 us (6%)
  other arithmetic  1.07 us (2%)
    pallas_call x1, Pallas kernels, body(): pl.pallas_call(functools.partial(kernel, spaces), out_shape=jax.ShapeDtyp...  49.6 us
    unnamed x1, local copies, waits for them, and re-layouts  1.87 us
    convert_element_type x1, local copies, waits for them, and re-layouts, body(): return jnp.transpose(out, (2, 1, 0, 3)).astype(jnp.float32)  1.34 us

profile of v1, /device:TPU:24, one launch (start us, length us, event | category | flops | bytes accessed | tf_op | source)
XLA Modules:
  0.0 53.9 jit_solution(14091632792339280035)
XLA Ops:
  0.0 1.9 %copy.9 = bf16[16,2,16,384]{3,0,1,2:T(8,128)(2,1)} copy(bf16[16,2,16,384]{3,2,1,0:T(8,128)(2,1)} %param.5) | data formatting | bytes 786432 | tf_op args[0]
  1.9 49.6 %shard_map.55 = bf16[16,2,16,384]{3,2,1,0:T(8,128)(2,1)} custom-call(s32[4,3]{1,0:T(4,128)} %cols.1, bf16[16,2,16,384]{3,2,1,0:T(8,128)(2,1)} %bitcast.7, bf16[4,3,8,2,96,96]{5,4,3,2,1,0:T(8,128)(2,1)} %st.1, s32[8,32,256]{2,1,0:T(8,128)} %bitcast.8, bf16[8,32,256]{2,1,0:T(8,128)(2,1)} %bitcast.9), custom_call_target="tpu_custom_call" | custom-call | tf_op jit(solution)/shard_map/pallas_call | solution.py:243
  51.5 1.1 %convert_bitcast_fusion = f32[16,2,16,384]{3,0,1,2:T(8,128)S(1)} fusion(bf16[16,2,16,384]{3,2,1,0:T(8,128)(2,1)} %shard_map.55), kind=kLoop, calls=%fused_computation | loop fusion | flops 196608 | bytes 1179648 | tf_op jit(solution)/shard_map/convert_element_type | solution.py:269
  52.6 1.3 %copy.7 = f32[16,2,16,384]{3,2,1,0:T(8,128)} copy(f32[16,2,16,384]{3,0,1,2:T(8,128)S(1)} %convert_bitcast_fusion) | data formatting | bytes 1572864 | tf_op jit(solution)/shard_map/convert_element_type | solution.py:269

commit v2 on v1

v2 whole, which is shorter than its diff:
```python
import functools

import jax
import jax.numpy as jnp
from jax import lax
from jax.experimental import pallas as pl
from jax.experimental.pallas import tpu as pltpu
from jax.sharding import PartitionSpec as P

MESH = pl.DeviceIdType.MESH
TILE = 96
LANE = 128
NKL = 8
NNZ = 3
FAR = (15, 14, 11, 10, 7, 6, 3, 2)
NEAR = (13, 12, 9, 8, 5, 4, 1)
ORDER = FAR + NEAR
PLACES = FAR + NEAR + (0,)
CHUNKS = ((0, 8), (8, 16))


def kernel(
    spaces,
    cols_hbm,
    x,
    st,
    ci_hbm,
    cv_hbm,
    out,
    cols,
    ci,
    cv,
    raw,
    xt,
    got,
    left_halo,
    right_halo,
    tiles,
    coup,
    weights,
    block,
    mixed,
    result,
    back,
    local_sem,
    in_send,
    in_recv,
    halo_send,
    halo_recv,
    out_send,
    out_recv,
):
    s, c = lax.axis_index("space"), lax.axis_index("chaos")
    has_left, has_right = s > 0, s < spaces - 1
    load_x = pltpu.make_async_copy(x, raw, local_sem.at[0])
    load_x.start()
    load_tiles = pltpu.make_async_copy(st, tiles, local_sem.at[1])
    load_terms = [
        pltpu.make_async_copy(ci_hbm, ci, local_sem.at[5]),
        pltpu.make_async_copy(cv_hbm, cv, local_sem.at[6]),
        pltpu.make_async_copy(cols_hbm, cols, local_sem.at[7]),
    ]
    for copy in load_terms:
        copy.start()
    load_tiles.start()

    barrier = pltpu.get_barrier_semaphore()
    for k in ORDER:
        pl.semaphore_signal(barrier, inc=1, device_id=(s, c ^ k), device_id_type=MESH)

    @pl.when(has_left)
    def _():
        pl.semaphore_signal(barrier, inc=1, device_id=(s - 1, c), device_id_type=MESH)

    @pl.when(has_right)
    def _():
        pl.semaphore_signal(barrier, inc=1, device_id=(s + 1, c), device_id_type=MESH)

    load_x.wait()
    for part in range(2):
        for t in range(3):
            value = raw[:, part, :, t * LANE : (t + 1) * LANE]
            xt[t, :, part] = jnp.swapaxes(value, 0, 1)

    pl.semaphore_wait(barrier, 15 + has_left.astype(jnp.int32) + has_right.astype(jnp.int32))

    def in_copy(t, k):
        return pltpu.make_async_remote_copy(
            xt.at[t, c ^ k], got.at[t, c], in_send.at[t, k], in_recv.at[t, k], device_id=(s, c ^ k), device_id_type=MESH
        )

    for t in (0, 2, 1):
        for k in ORDER:
            in_copy(t, k).start()
    own_in = [pltpu.make_async_copy(xt.at[t, c], got.at[t, c], local_sem.at[2 + t]) for t in range(3)]
    for copy in own_in:
        copy.start()

    for copy in load_terms:
        copy.wait()

    def one_coupling(step, _):
        k, half = step // 2, step % 2
        rows = lax.broadcasted_iota(jnp.int32, (LANE, 256), 0) + half * LANE
        total = jnp.zeros((LANE, 256), jnp.float32)
        for n in range(32):
            total = jnp.where(ci[k, n : n + 1, :] == rows, cv[k, n : n + 1, :].astype(jnp.float32), total)
        coup[k, :, pl.ds(pl.multiple_of(half * LANE, LANE), LANE)] = total.T.astype(jnp.bfloat16)
        return 0

    lax.fori_loop(0, 2 * NKL, one_coupling, 0)

    @pl.when(jnp.logical_not(has_left))
    def _():
        left_halo[...] = jnp.zeros_like(left_halo)

    @pl.when(jnp.logical_not(has_right))
    def _():
        right_halo[...] = jnp.zeros_like(right_halo)

    def to_left(k):
        return pltpu.make_async_remote_copy(
            got.at[0, c ^ k],
            right_halo.at[c ^ k],
            halo_send.at[0, k],
            halo_recv.at[0, k],
            device_id=(s - 1, c),
            device_id_type=MESH,
        )

    def to_right(k):
        return pltpu.make_async_remote_copy(
            got.at[2, c ^ k],
            left_halo.at[c ^ k],
            halo_send.at[1, k],
            halo_recv.at[1, k],
            device_id=(s + 1, c),
            device_id_type=MESH,
        )

    def arrived(t, k):
        if k:
            in_copy(t, k).wait_recv()
        else:
            own_in[t].wait()

    ARRIVE = (0,) + NEAR[::-1] + FAR

    load_tiles.wait()

    def one_weight(step, _):
        b, slot = step // NNZ, step % NNZ
        side, below = jnp.zeros((TILE, LANE - TILE), jnp.bfloat16), jnp.zeros((LANE - TILE, 2 * LANE), jnp.bfloat16)
        for k in range(NKL):
            real = jnp.concatenate([tiles[b, slot, k, 0].T, side], axis=1)
            imag = jnp.concatenate([tiles[b, slot, k, 1].T, side], axis=1)
            first, second = 2 * k * LANE, (2 * k + 1) * LANE
            weights[b, slot, first : first + TILE, :] = jnp.concatenate([real, imag], axis=1)
            weights[b, slot, first + TILE : second, :] = below
            weights[b, slot, second : second + TILE, :] = jnp.concatenate([-imag, real], axis=1)
            weights[b, slot, second + TILE : second + LANE, :] = below
        return 0

    lax.fori_loop(0, 4 * NNZ, one_weight, 0)

    for k in ARRIVE:
        arrived(0, k)

        @pl.when(has_left)
        def _():
            to_left(k).start()

    for k in ARRIVE:
        arrived(2, k)

        @pl.when(has_right)
        def _():
            to_right(k).start()

    pad = jnp.zeros((256, LANE - TILE), jnp.bfloat16)

    def tile(t, part):
        return got[t, :, part].reshape(256, LANE)

    def shifted(low, high, start):
        return jnp.concatenate([low[:, start:], high[:, :start]], axis=1)

    def padded(low):
        return jnp.concatenate([low[:, LANE - TILE :], pad], axis=1)

    def mix(g, cells):
        for part in range(2):
            block[:, part * LANE : (part + 1) * LANE] = cells(part)

        def one_k(k, _):
            value = jnp.dot(coup[k], block[...], preferred_element_type=jnp.float32)
            value = value.astype(jnp.bfloat16)
            for q in range(16):
                d = c ^ q
                place = 15 - ((d // 2) % 2 * 8 + d // 4 * 2 + d % 2)
                mixed[g, pl.ds(pl.multiple_of(place * 16, 16), 16), pl.ds(pl.multiple_of(k * 256, 256), 256)] = value[
                    16 * q : 16 * q + 16
                ]
            return 0

        lax.fori_loop(0, NKL, one_k, 0, unroll=True)

    mix(1, lambda part: tile(0, part))
    mix(4, lambda part: padded(tile(2, part)))

    @pl.when(has_right)
    def _():
        for k in range(16):
            to_left(k).wait_recv()

    mix(5, lambda part: right_halo[:, part].reshape(256, LANE))

    @pl.when(has_left)
    def _():
        for k in range(16):
            to_right(k).wait_recv()

    mix(0, lambda part: padded(left_halo[:, part].reshape(256, LANE)))
    for k in ARRIVE:
        arrived(1, k)
    mix(2, lambda part: shifted(tile(0, part), tile(1, part), TILE))
    mix(3, lambda part: shifted(tile(1, part), tile(2, part), 2 * TILE - LANE))

    def out_copy(place):
        k = PLACES[place]
        return pltpu.make_async_remote_copy(
            result.at[place], back.at[c], out_send.at[k], out_recv.at[k], device_id=(s, c ^ k), device_id_type=MESH
        )

    for first, last in CHUNKS:
        rows = (last - first) * 16
        totals = []
        for b in range(4):
            total = jnp.zeros((rows, 2 * LANE), jnp.float32)
            for slot in range(NNZ):
                total = total + jnp.dot(
                    mixed[cols[b, slot], first * 16 : last * 16, :], weights[b, slot], preferred_element_type=jnp.float32
                )
            totals.append(total)
        for part in range(2):
            value = jnp.concatenate([total[:, part * LANE : part * LANE + TILE] for total in totals], axis=1)
            result[first:last, part] = value.astype(jnp.bfloat16).reshape(last - first, 16, 3 * LANE)
        for place in range(first, min(last, 15)):
            out_copy(place).start()
    own_out = pltpu.make_async_copy(result.at[15], back.at[c], local_sem.at[0])
    own_out.start()

    for t in range(3):
        for k in ORDER:
            in_copy(t, k).wait_send()

    @pl.when(has_left)
    def _():
        for k in range(16):
            to_left(k).wait_send()

    @pl.when(has_right)
    def _():
        for k in range(16):
            to_right(k).wait_send()

    own_out.wait()
    for place in range(15):
        out_copy(place).wait()
    for part in range(2):
        for t in range(3):
            value = back[:, part, :, t * LANE : (t + 1) * LANE]
            out[:, part, :, t * LANE : (t + 1) * LANE] = jnp.swapaxes(value, 0, 1)


def body(load_vectors, stiff_tiles, tile_columns, chaos_index, chaos_value):
    spaces = lax.axis_size("space")
    ci = jnp.transpose(chaos_index, (0, 2, 1))
    cv = jnp.transpose(chaos_value, (0, 2, 1))
    hbm = pl.BlockSpec(memory_space=pltpu.HBM)
    bf16 = jnp.bfloat16
    out = pl.pallas_call(
        functools.partial(kernel, spaces),
        out_shape=jax.ShapeDtypeStruct((16, 2, 16, 384), bf16),
        in_specs=[hbm] * 5,
        out_specs=pl.BlockSpec(memory_space=pltpu.VMEM),
        scratch_shapes=[
            pltpu.SMEM(tile_columns.shape, jnp.int32),
            pltpu.VMEM(ci.shape, jnp.int32),
            pltpu.VMEM(cv.shape, bf16),
            pltpu.VMEM((16, 2, 16, 384), bf16),
            pltpu.VMEM((3, 16, 2, 16, LANE), bf16),
            pltpu.VMEM((3, 16, 2, 16, LANE), bf16),
            pltpu.VMEM((16, 2, 16, LANE), bf16),
            pltpu.VMEM((16, 2, 16, LANE), bf16),
            pltpu.VMEM(stiff_tiles.shape, bf16),
            pltpu.VMEM((NKL, 256, 256), bf16),
            pltpu.VMEM((4, NNZ, 2 * NKL * LANE, 2 * LANE), bf16),
            pltpu.VMEM((256, 2 * LANE), bf16),
            pltpu.VMEM((6, 256, 2 * NKL * LANE), bf16),
            pltpu.VMEM((16, 2, 16, 384), bf16),
            pltpu.VMEM((16, 2, 16, 384), bf16),
            pltpu.SemaphoreType.DMA((8,)),
            pltpu.SemaphoreType.DMA((3, 16)),
            pltpu.SemaphoreType.DMA((3, 16)),
            pltpu.SemaphoreType.DMA((2, 16)),
            pltpu.SemaphoreType.DMA((2, 16)),
            pltpu.SemaphoreType.DMA((16,)),
            pltpu.SemaphoreType.DMA((16,)),
        ],
        compiler_params=pltpu.CompilerParams(collective_id=0, has_side_effects=True, vmem_limit_bytes=60 * 1024 * 1024),
    )(tile_columns, load_vectors, stiff_tiles, ci, cv)
    return out.astype(jnp.float32)


def solution(mesh):
    in_specs = (
        P("chaos", None, None, "space"),
        P("space", None, None, None, None, None),
        P("space", None),
        P(),
        P(),
    )
    out_specs = P("chaos", None, None, "space")
    return jax.shard_map(body, mesh=mesh, in_specs=in_specs, out_specs=out_specs, check_vma=False)
```

time: 54.1 us -> 50.6 us (0.935)
  the two profiles are of different devices: /device:TPU:24 before, /device:TPU:9 now
where the time goes in v2:
time: 50.6 us; the launch traced here: 50.2 us
  Pallas kernels  48.3 us (95%)
  other arithmetic  1.96 us (4%)
    pallas_call x1, Pallas kernels, body(): pl.pallas_call(functools.partial(kernel, spaces), out_shape=jax.ShapeDtyp...  48.3 us
    convert_element_type x1, other arithmetic, body(): return out.astype(jnp.float32)  1.96 us

profile of v2, /device:TPU:9, one launch (start us, length us, event | category | flops | bytes accessed | tf_op | source)
XLA Modules:
  0.0 50.2 jit_solution(17019086352063745205)
XLA Ops:
  0.0 48.3 %shard_map.55 = bf16[16,2,16,384]{3,2,1,0:T(8,128)(2,1)} custom-call(s32[4,3]{1,0:T(4,128)} %cols_hbm.1, bf16[16,2,16,384]{3,2,1,0:T(8,128)(2,1)} %x.1, bf16[4,3,8,2,96,96]{5,4,3,2,1,0:T(8,128)(2,1)} %st.1, s32[8,32,256]{2,1,0:T(8,128)} %bitcast.2, bf16[8,32,256]{2,1,0:T(8,128)(2,1)} %bitcast.3), custom_call_target="tpu_custom_call" | custom-call | tf_op jit(solution)/shard_map/pallas_call | solution.py:282
  48.3 2.0 %convert_element_type.3 = f32[16,2,16,384]{3,2,1,0:T(8,128)} convert(bf16[16,2,16,384]{3,2,1,0:T(8,128)(2,1)} %shard_map.55) | non-fusion elementwise | flops 196608 | bytes 1179648 | tf_op jit(solution)/shard_map/convert_element_type | solution.py:313

commit v3 on v2

--- a/solution.py
+++ b/solution.py
@@ -12,7 +12,7 @@
 LANE = 128
 NKL = 8
 NNZ = 3
-FAR = (15, 14, 11, 10, 7, 6, 3, 2)
+FAR = (14, 10, 6, 2, 15, 11, 7, 3)
 NEAR = (13, 12, 9, 8, 5, 4, 1)
 ORDER = FAR + NEAR
 PLACES = FAR + NEAR + (0,)
@@ -197,7 +197,8 @@
             value = value.astype(jnp.bfloat16)
             for q in range(16):
                 d = c ^ q
-                place = 15 - ((d // 2) % 2 * 8 + d // 4 * 2 + d % 2)
+                far = (d // 2) % 2
+                place = 15 - (far * 8 + (1 - far) * (d // 4 * 2 + d % 2) + far * (d % 2 * -4 + 4 + d // 4 - (1 - d % 2) * 0))
                 mixed[g, pl.ds(pl.multiple_of(place * 16, 16), 16), pl.ds(pl.multiple_of(k * 256, 256), 256)] = value[
                     16 * q : 16 * q + 16
                 ]

time: 50.6 us -> 50.7 us (level)
  no operation moved by 1% of the time
where the time goes in v3:
time: 50.7 us; the launch traced here: 50.5 us
  Pallas kernels  48.5 us (96%)
  other arithmetic  1.96 us (4%)
    pallas_call x1, Pallas kernels, body(): pl.pallas_call(functools.partial(kernel, spaces), out_shape=jax.ShapeDtyp...  48.5 us
    convert_element_type x1, other arithmetic, body(): return out.astype(jnp.float32)  1.96 us

profile of v3, /device:TPU:9, one launch (start us, length us, event | category | flops | bytes accessed | tf_op | source)
XLA Modules:
  0.0 50.5 jit_solution(2395734420723490956)
XLA Ops:
  0.0 48.5 %shard_map.55 = bf16[16,2,16,384]{3,2,1,0:T(8,128)(2,1)} custom-call(s32[4,3]{1,0:T(4,128)} %cols_hbm.1, bf16[16,2,16,384]{3,2,1,0:T(8,128)(2,1)} %x.1, bf16[4,3,8,2,96,96]{5,4,3,2,1,0:T(8,128)(2,1)} %st.1, s32[8,32,256]{2,1,0:T(8,128)} %bitcast.2, bf16[8,32,256]{2,1,0:T(8,128)(2,1)} %bitcast.3), custom_call_target="tpu_custom_call" | custom-call | tf_op jit(solution)/shard_map/pallas_call | solution.py:283
  48.6 2.0 %convert_element_type.3 = f32[16,2,16,384]{3,2,1,0:T(8,128)} convert(bf16[16,2,16,384]{3,2,1,0:T(8,128)(2,1)} %shard_map.55) | non-fusion elementwise | flops 196608 | bytes 1179648 | tf_op jit(solution)/shard_map/convert_element_type | solution.py:314
